TPU v7x, 256 devices: a whole 4x4x8 slice. The times are simulated.
256 devices in a mesh: row: 32 (over z_lo, y, core), col: 8 (over z_hi, x).
Axes of the slice: x: 4, y: 4, z: 8 (z_hi: 2, z_lo: 4; z = z_hi * 4 + z_lo), core: 2. Of those that a mesh axis runs over, the one named last changes fastest.
Arguments:
- weights: bfloat16 [8192, 32768], P('row', 'col'), may hold values from -6 to 6
- panel_first: float32 [256, 32768], P('row', 'col'), may hold values from -1 to 2, as said below
- panel_second: float32 [256, 32768], P('row', 'col'), may hold values from -1 to 2, as said below
- removed_first: int32 [512], P('col'), may hold values from -1 to 4095, as said below
- removed_second: int32 [512], P('col'), may hold values from -1 to 4095, as said below
Outputs:
- pruned: bfloat16 [8192, 32768], P('row', 'col')
Inputs may be any that keep to these rules, and one draw needn't show every extreme that they name: `removed_first`: in each list every owner's live slots come first; there are 256 live slots in all, at most 64 for one owner and exactly 64 for some owner; live values of one owner are distinct, and the two lists name no column twice. `removed_second`: same form as removed_first, with its own owners. `panel_first`: together with panel_second, its entries at the columns S1 and S2 are the rows of one symmetric positive definite matrix of order 2 * 256. `panel_second`: rows of the same inverse Hessian as panel_first, for the columns S2.
All inputs are finite; a program needn't handle non-finite values.
Results may differ from a plain program's by a relative error of at most 0.001.
Values may be sent and summed in bfloat16 or wider, within the bound.
No kernel may reach another device: no remote copies, remote signals or barrier semaphores. Data moves between devices by JAX's collectives and lax.ppermute only.
A program may use at most 64 MiB of HBM per device.

v0:
```python
import jax
import jax.numpy as jnp
from jax import lax
from jax.sharding import PartitionSpec as P

highest = lax.Precision.HIGHEST


def pick_columns(matrix, chosen):
    present = chosen >= 0
    column = jnp.where(present, chosen, 0)
    taken = jnp.take(matrix, column, axis=1)
    return jnp.where(present[None, :], taken, jnp.zeros((), matrix.dtype))


def compactor(gathered, total):
    present = gathered >= 0
    position = jnp.cumsum(present.astype(jnp.int32)) - 1
    target = jnp.arange(total, dtype=jnp.int32)
    return (present[:, None] & (position[:, None] == target[None, :])).astype(jnp.float32)


def apply_inverse(factor, matrix):
    return jax.scipy.linalg.cho_solve((factor, True), matrix.T).T


def on_device(weights, panel_first, panel_second, removed_first, removed_second):
    panel_rows = panel_first.shape[0]
    slot_count = removed_first.shape[0]
    row_devices = lax.axis_size("row")
    col_devices = lax.axis_size("col")
    order = panel_rows * row_devices
    lists_first, lists_second = (
        lax.all_gather(removed_first, "col", axis=0, tiled=True),
        lax.all_gather(removed_second, "col", axis=0, tiled=True),
    )
    pack_first = compactor(lists_first, order)
    pack_second = compactor(lists_second, order)
    stacked = jnp.stack([panel_first, panel_second])
    chosen = jnp.concatenate([removed_first, removed_second])
    present = chosen >= 0
    column = jnp.where(present, chosen, 0)
    local_entries = jnp.where(present[None, None, :], jnp.take(stacked, column, axis=2), 0.0)
    everyone = lax.all_gather(local_entries[None], ("row", "col"), axis=0, tiled=True)
    everyone = everyone.reshape(row_devices, col_devices, 2, panel_rows, 2, slot_count)
    everyone = jnp.transpose(everyone, (2, 4, 0, 3, 1, 5)).reshape(
        2, 2, order, col_devices * slot_count
    )
    h_first = jnp.dot(everyone[0, 0], pack_first, precision=highest)
    first_at_second = jnp.dot(everyone[0, 1], pack_second, precision=highest)
    second_at_first = jnp.dot(everyone[1, 0], pack_first, precision=highest)
    second_at_second = jnp.dot(everyone[1, 1], pack_second, precision=highest)
    factor_first = jnp.linalg.cholesky(h_first)
    coupling = apply_inverse(factor_first, second_at_first)
    h_second = second_at_second - jnp.dot(coupling, first_at_second, precision=highest)
    factor_second = jnp.linalg.cholesky(h_second)
    first_local = pick_columns(weights, removed_first)
    first_cols = lax.all_gather(first_local, "col", axis=1, tiled=True)
    w_first = jnp.dot(
        first_cols, pack_first.astype(jnp.bfloat16), preferred_element_type=jnp.float32
    )
    coef_first = apply_inverse(factor_first, w_first)
    panel_whole = lax.all_gather(panel_first, "row", axis=0, tiled=True)
    updated = weights.astype(jnp.float32) - jnp.dot(coef_first, panel_whole, precision=highest)
    panel_next = lax.all_gather(panel_second, "row", axis=0, tiled=True) - jnp.dot(
        coupling, panel_whole, precision=highest
    )
    second_local = pick_columns(updated, removed_second)
    second_cols = lax.all_gather(second_local, "col", axis=1, tiled=True)
    w_second = jnp.dot(second_cols, pack_second, precision=highest)
    coef_second = apply_inverse(factor_second, w_second)
    pruned = updated - jnp.dot(coef_second, panel_next, precision=highest)
    return pruned.astype(jnp.bfloat16)


def solution(mesh):
    return jax.shard_map(
        on_device,
        mesh=mesh,
        in_specs=(P("row", "col"), P("row", "col"), P("row", "col"), P("col"), P("col")),
        out_specs=P("row", "col"),
        check_vma=False,
    )
```

profile of v0, /device:TPU:1, one launch (start us, length us, event | category | flops | bytes accessed | tf_op | source)
XLA Modules:
  0.0 960.8 jit_solution(7421695014664704210)
XLA Ops:
  7.7 4.4 copy.21
  12.2 2.9 gather_fusion
  19.5 15.6 %all-reduce.3 = (s32[512]{0:T(512)S(1)}, s32[512]{0:T(512)S(1)}) all-reduce(s32[512]{0:T(512)S(1)} %dynamic-update-slice.10, s32[512]{0:T(512)S(1)} %dynamic-update-slice.11), channel_id=1, replica_groups=mesh['row'=32,'col'=8] {'col'}, use_global_device_ids=true, to_apply=%add.1 | all-reduce | flops 1024 | bytes 8192
  36.3 2.5 copy.25
  38.8 2.5 gather_fusion.1
  41.4 37.7 %all_gather.23 = bf16[256,512]{0,1:T(8,128)(2,1)S(1)} all-gather(bf16[256,64]{0,1:T(8,128)(2,1)S(1)} %select_bitcast_fusion.3), channel_id=1, replica_groups=mesh['row'=32,'col'=8] {'col'}, dimensions={1}, use_global_device_ids=true | all-gather | bytes 294912 | tf_op jit(solution)/shard_map/all_gather | solution.py:58
  80.2 655.8 %all-gather.4.cloned.1.call-done = f32[256,2,8,128]{3,2,1,0:T(8,128)} async-done(((f32[1,2,8,128]{3,2,1,0:T(8,128)}), f32[256,2,8,128]{3,2,1,0:T(8,128)}) %all-gather.4.cloned.1.call-update) | async-done | bytes 2097168 | tf_op jit(solution)/shard_map/all_gather | solution.py:44
  736.0 5.6 reshape.193
  741.6 6.6 copy.33
  748.2 3.9 reshape.194
  753.5 11.7 %cholesky.130 = f32[128,128]{1,0:T(8,128)S(1)} custom-call(f32[128,128]{1,0:T(8,128)S(1)} %cholesky.194), custom_call_target="Cholesky" | custom-call | tf_op jit(solution)/shard_map/jit(cholesky)/cholesky | solution.py:53
  765.3 9.8 %custom-call.16 = f32[1,128,128]{1,2,0:T(8,128)S(1)} custom-call(f32[1,128,128]{2,1,0:T(8,128)S(1)} %get-tuple-element.67), custom_call_target="InvertDiagBlocksLowerTriangular" | custom-call | tf_op jit(solution)/shard_map/jit(cholesky)/cholesky | solution.py:53
  775.6 11.7 %cholesky.147 = f32[128,128]{1,0:T(8,128)S(1)} custom-call(f32[128,128]{1,0:T(8,128)S(1)} %convolution_subtract_fusion.11), custom_call_target="Cholesky" | custom-call | tf_op jit(solution)/shard_map/jit(cholesky)/cholesky | solution.py:53
  789.3 3.7 while.6
  789.9 1.3 bitcast_dynamic-update-slice_fusion.4
  791.7 1.3 bitcast_dynamic-update-slice_fusion.4
  793.0 19.8 %custom-call.17 = f32[2,128,128]{1,2,0:T(8,128)S(1)} custom-call(f32[2,128,128]{2,1,0:T(8,128)S(1)} %get-tuple-element.27), custom_call_target="InvertDiagBlocksLowerTriangular" | custom-call | tf_op jit(solution)/shard_map/jit(_cho_solve)/triangular_solve | solution.py:24
  817.5 11.7 %cholesky.164 = f32[128,128]{1,0:T(8,128)S(1)} custom-call(f32[128,128]{1,0:T(8,128)S(1)} %cholesky.197), custom_call_target="Cholesky" | custom-call | tf_op jit(solution)/shard_map/jit(cholesky)/cholesky | solution.py:56
  829.3 9.8 %custom-call.19 = f32[1,128,128]{1,2,0:T(8,128)S(1)} custom-call(f32[1,128,128]{2,1,0:T(8,128)S(1)} %get-tuple-element.63), custom_call_target="InvertDiagBlocksLowerTriangular" | custom-call | tf_op jit(solution)/shard_map/jit(cholesky)/cholesky | solution.py:56
  841.2 11.9 %cholesky.181 = f32[128,128]{1,0:T(8,128)S(1)} custom-call(f32[128,128]{1,0:T(8,128)S(1)} %convolution_subtract_fusion.10), custom_call_target="Cholesky" | custom-call | tf_op jit(solution)/shard_map/jit(cholesky)/cholesky | solution.py:56
  855.7 3.7 while.7
  856.3 1.3 bitcast_dynamic-update-slice_fusion.5
  858.2 1.3 bitcast_dynamic-update-slice_fusion.5
  859.5 19.7 %custom-call.20 = f32[2,128,128]{1,2,0:T(8,128)S(1)} custom-call(f32[2,128,128]{2,1,0:T(8,128)S(1)} %get-tuple-element.29), custom_call_target="InvertDiagBlocksLowerTriangular" | custom-call | tf_op jit(solution)/shard_map/jit(_cho_solve)/triangular_solve | solution.py:24
  879.1 1.2 fusion.39
  880.4 1.2 convolution_subtract_fusion.9
  882.7 8.3 convolution_subtract_fusion.2
  891.0 5.6 copy.29
  896.6 2.8 gather_fusion.2
  899.6 38.7 %all_gather.26 = f32[256,512]{0,1:T(8,128)S(1)} all-gather(f32[256,64]{0,1:T(8,128)S(1)} %select_bitcast_fusion.2), channel_id=1, replica_groups=mesh['row'=32,'col'=8] {'col'}, dimensions={1}, use_global_device_ids=true | all-gather | bytes 589824 | tf_op jit(solution)/shard_map/all_gather | solution.py:69
  940.8 8.1 convolution_subtract_fusion.1
  948.9 5.1 fusion
  (107 shorter events, 24.0 us)
Async XLA Ops:
  6.5 11.2 %copy-start.6 = (u32[256]{0:T(256)S(1)}, u32[256]{0:T(256)}, u32[]{:S(2)}) copy-start(u32[256]{0:T(256)} %constant.149) | copy-start | bytes 3076
  6.5 5.5 copy-start.4
  6.5 5.5 copy-start.5
  6.5 29.8 %copy-start.1 = (bf16[256,4096]{1,0:T(8,128)(2,1)S(1)}, bf16[256,4096]{1,0:T(8,128)(2,1)}, u32[]{:S(2)}) copy-start(bf16[256,4096]{1,0:T(8,128)(2,1)} %param.8) | copy-start | bytes 6291460
  6.5 729.5 %all-gather.4.cloned.1.call-start = ((), (), s32[]{:S(2)}) async-start(), calls=%async_computation | async-start | bytes 2105344 | tf_op jit(solution)/shard_map/all_gather | solution.py:44
  16.2 866.5 %all-gather.6.cloned.1.call-start = ((), (), s32[]{:S(2)}) async-start(), calls=%async_computation.1 | async-start | bytes 4325376 | tf_op jit(solution)/shard_map/all_gather | solution.py:63
  17.0 923.8 %all-gather.8.cloned.1.call-start = ((), (), s32[]{:S(2)}) async-start(), calls=%async_computation.2 | async-start | bytes 4325376 | tf_op jit(solution)/shard_map/all_gather | solution.py:65
  816.0 66.8 %copy-start.2 = (bf16[256,4096]{1,0:T(8,128)(2,1)S(1)}, bf16[256,4096]{1,0:T(8,128)(2,1)}, u32[]{:S(2)}) copy-start(bf16[256,4096]{1,0:T(8,128)(2,1)} %param.8) | copy-start | bytes 6291460
  816.8 0.7 copy-start.3
  940.8 8.1 copy-start
Sparse Core Ops, SparseCore 0:
  16.4 719.6 all-gather.3
  737.9 62.2 all-gather.5
  802.1 62.1 all-gather.7
where the time goes:
time: 977 us; the launch traced here: 961 us
  waiting for transfers between devices  657 us (67%)
  other arithmetic  111 us (11%)
  blocking collectives  91.9 us (9%)
  local copies, waits for them, and re-layouts  47.5 us (5%)
  matrix products  35.9 us (4%)
  between operations  16.9 us (2%)
    all_gather x1, waiting for transfers between devices, on_device(): lax.all_gather(local_entries[None], ('row', 'col'), axis=0, tiled=True)  656 us
    another operation x5, other arithmetic, apply_inverse(): return jax.scipy.linalg.cho_solve((factor, True), matrix.T).T  39.6 us
    all_gather x1, blocking collectives, on_device(): second_cols = lax.all_gather(second_local, 'col', axis=1, tiled=True)  38.7 us
    all_gather x1, blocking collectives, on_device(): first_cols = lax.all_gather(first_local, 'col', axis=1, tiled=True)  37.7 us
    another operation x7, other arithmetic, on_device(): factor_second = jnp.linalg.cholesky(h_second)  34.7 us
    another operation x6, other arithmetic, on_device(): factor_first = jnp.linalg.cholesky(h_first)  34 us
  transfers between devices with their start and end apart: 3, of which 1 were waited for; matrix products, arithmetic and copies ran while one was open for 18% of the time, Pallas kernels for 0%

commit v1 on v0

v1 whole, which is shorter than its diff:
```python
import jax
import jax.numpy as jnp
from jax import lax
from jax.experimental import pallas as pl
from jax.experimental.pallas import tpu as pltpu
from jax.sharding import PartitionSpec as P

f32 = jnp.float32
bf16 = jnp.bfloat16
VMEM = pltpu.VMEM
TOLERANCE = 3e-5
DOUBLINGS = 6


def vmem_spec():
    return pl.BlockSpec(memory_space=VMEM)


def halves(value):
    high = value.astype(bf16)
    low = (value - high.astype(f32)).astype(bf16)
    return high, low


def dot(a, b):
    return jnp.dot(a, b, preferred_element_type=f32)


def product(a, b):
    a_high, a_low = halves(a)
    b_high, b_low = halves(b)
    return dot(a_high, b_high) + (dot(a_high, b_low) + dot(a_low, b_high))


def extract_kernel(weights_ref, panels_ref, chosen_ref, out_ref, acc):
    step = pl.program_id(0)
    tile = weights_ref.shape[1]
    rows = weights_ref.shape[0]
    height = panels_ref.shape[0]

    @pl.when(step == 0)
    def _():
        acc[...] = jnp.zeros_like(acc)

    chosen = chosen_ref[...]
    column = lax.broadcasted_iota(jnp.int32, (tile, chosen.shape[1]), 0) + step * tile
    onehot = (column == chosen).astype(f32).astype(bf16)
    panels = panels_ref[...]
    high = panels.astype(bf16)
    rest = panels - high.astype(f32)
    middle = rest.astype(bf16)
    low = (rest - middle.astype(f32)).astype(bf16)
    acc[0:rows, :] += dot(weights_ref[...], onehot)
    acc[rows : rows + 3 * height, :] += dot(jnp.concatenate([high, middle, low], axis=0), onehot)

    @pl.when(step == pl.num_programs(0) - 1)
    def _():
        acc[rows + 3 * height :, :] = jnp.broadcast_to(
            (chosen >= 0).astype(f32), (height, chosen.shape[1])
        )
        out_ref[...] = acc[...].astype(bf16)


def extract(weights, panels, chosen):
    rows, width = weights.shape
    height = panels.shape[0]
    tile = 1024
    slots = chosen.shape[1]
    total = rows + 4 * height
    return pl.pallas_call(
        extract_kernel,
        out_shape=jax.ShapeDtypeStruct((total, slots), bf16),
        grid=(width // tile,),
        in_specs=[
            pl.BlockSpec((rows, tile), lambda i: (0, i)),
            pl.BlockSpec((height, tile), lambda i: (0, i)),
            pl.BlockSpec((1, slots), lambda i: (0, 0)),
        ],
        out_specs=pl.BlockSpec((total, slots), lambda i: (0, 0)),
        scratch_shapes=[VMEM((total, slots), f32)],
        name="extract",
    )(weights, panels, chosen)


def compact_kernel(slots_ref, columns_ref, entries_ref, acc):
    owners, total, slots = slots_ref.shape
    order = entries_ref.shape[1]
    height = entries_ref.shape[0]
    rows = columns_ref.shape[0]
    half = slots // 2
    lane = lax.broadcasted_iota(jnp.int32, (1, slots), 1)
    in_second = lane >= half
    slot = jnp.where(in_second, lane - half, lane)
    target = lax.broadcasted_iota(jnp.int32, (order, slots), 0)
    per_list = order // 2
    per_device = height // 2
    base_first = jnp.zeros((1, 1), f32)
    base_second = jnp.zeros((1, 1), f32)
    for owner in range(owners):
        live = slots_ref[owner, total - height : total, :].astype(f32)[0:1, :]
        start = jnp.where(in_second, base_second, base_first).astype(jnp.int32)
        position = start + slot
        place = (
            (position // per_device) * height
            + jnp.where(in_second, per_device, 0)
            + position % per_device
        )
        place = jnp.where(live > 0.5, place, -1)
        move = (target == place).astype(f32).astype(bf16)
        share = lax.dot_general(
            slots_ref[owner, 0 : total - height, :],
            move,
            (((1,), (1,)), ((), ())),
            preferred_element_type=f32,
        )
        if owner == 0:
            acc[...] = share
        else:
            acc[...] += share
        base_first = base_first + jnp.sum(jnp.where(in_second, 0.0, live), axis=1, keepdims=True)
        base_second = base_second + jnp.sum(jnp.where(in_second, live, 0.0), axis=1, keepdims=True)
    columns_ref[...] = acc[0:rows, :].astype(bf16)
    high = acc[rows : rows + height, :]
    middle = acc[rows + height : rows + 2 * height, :]
    low = acc[rows + 2 * height : rows + 3 * height, :]
    entries_ref[...] = high + (middle + low)


def compact(received, rows, height, order):
    return pl.pallas_call(
        compact_kernel,
        out_shape=(
            jax.ShapeDtypeStruct((rows, order), bf16),
            jax.ShapeDtypeStruct((height, order), f32),
        ),
        in_specs=[vmem_spec()],
        out_specs=(vmem_spec(), vmem_spec()),
        scratch_shapes=[VMEM((rows + 3 * height, order), f32)],
        name="compact",
    )(received)


def solve_kernel(entries_ref, columns_ref, high_ref, low_ref, stacked, inverse):
    order = entries_ref.shape[0]
    rows = columns_ref.shape[0]
    row = lax.broadcasted_iota(jnp.int32, (order, order), 0)
    col = lax.broadcasted_iota(jnp.int32, (order, order), 1)
    entries = entries_ref[...]
    diagonal = jnp.where(row == col, entries, 0.0)
    scale_row = lax.rsqrt(jnp.sum(diagonal, axis=0, keepdims=True))
    scale_col = lax.rsqrt(jnp.sum(diagonal, axis=1, keepdims=True))
    unit = entries * scale_col * scale_row
    rest = jnp.where(row == col, 1.0 - unit, -unit)
    stacked[0:rows, :] = columns_ref[...].astype(f32) * scale_row
    stacked[rows:, :] = rest

    def bound():
        power = stacked[rows:, :]
        return jnp.sum(power * power)

    def going(state):
        count, left = state
        return jnp.logical_and(count < DOUBLINGS, jnp.logical_not(left < TOLERANCE))

    def double(state):
        count, _ = state
        power = stacked[rows:, :]
        result = product(stacked[...], power)
        stacked[0:rows, :] += result[0:rows, :]
        stacked[rows:, :] = result[rows:, :]
        return count + 1, bound()

    _, left = lax.while_loop(going, double, (jnp.int32(0), bound()))
    settled = left < TOLERANCE

    @pl.when(settled)
    def _():
        solved = stacked[0:rows, :]
        solved = (solved + product(solved, stacked[rows:, :])) * scale_row
        high, low = halves(solved)
        high_ref[...] = high
        low_ref[...] = low

    @pl.when(jnp.logical_not(settled))
    def _():
        inverse[...] = entries_ref[...] * scale_col * scale_row

        def pivot(k, carry):
            lanes = lax.broadcasted_iota(jnp.int32, (1, order), 1)
            pivot_row = inverse[pl.ds(k, 1), :]
            head = jnp.sum(jnp.where(lanes == k, pivot_row, 0.0), axis=1, keepdims=True)
            pivot_row = jnp.where(lanes == k, 1.0, pivot_row) / head
            everything = inverse[...]
            column = jnp.sum(jnp.where(col == k, everything, 0.0), axis=1, keepdims=True)
            kept = jnp.where(col == k, 0.0, everything)
            inverse[...] = kept - column * pivot_row
            inverse[pl.ds(k, 1), :] = pivot_row
            return carry

        lax.fori_loop(0, order, pivot, 0)
        whole = entries_ref[...] * scale_col * scale_row
        wanted = columns_ref[...].astype(f32) * scale_row

        def exact(a, b):
            return jnp.dot(a, b, precision=lax.Precision.HIGHEST, preferred_element_type=f32)

        solved = exact(wanted, inverse[...])
        solved = solved + exact(wanted - exact(solved, whole), inverse[...])
        high, low = halves(solved * scale_row)
        high_ref[...] = high
        low_ref[...] = low


def solve(entries, columns):
    rows, order = columns.shape
    return pl.pallas_call(
        solve_kernel,
        out_shape=(jax.ShapeDtypeStruct((rows, order), bf16),) * 2,
        in_specs=[vmem_spec(), vmem_spec()],
        out_specs=(vmem_spec(), vmem_spec()),
        scratch_shapes=[VMEM((rows + order, order), f32), VMEM((order, order), f32)],
        name="solve",
    )(entries, columns)


def update_kernel(weights_ref, panels_ref, high_ref, low_ref, out_ref):
    panel_high, panel_low = halves(panels_ref[...])
    high = high_ref[...]
    change = dot(high, panel_high) + (dot(high, panel_low) + dot(low_ref[...], panel_high))
    out_ref[...] = (weights_ref[...].astype(f32) - change).astype(bf16)


def update(weights, panels, high, low):
    rows, width = weights.shape
    order = panels.shape[0]
    tile = 512
    return pl.pallas_call(
        update_kernel,
        out_shape=jax.ShapeDtypeStruct((rows, width), bf16),
        grid=(width // tile,),
        in_specs=[
            pl.BlockSpec((rows, tile), lambda i: (0, i)),
            pl.BlockSpec((order, tile), lambda i: (0, i)),
            pl.BlockSpec((rows, order), lambda i: (0, 0)),
            pl.BlockSpec((rows, order), lambda i: (0, 0)),
        ],
        out_specs=pl.BlockSpec((rows, tile), lambda i: (0, i)),
        name="update",
    )(weights, panels, high, low)


def on_device(weights, panel_first, panel_second, removed_first, removed_second):
    rows = weights.shape[0]
    row_devices = lax.axis_size("row")
    col_devices = lax.axis_size("col")
    panels = jnp.concatenate([panel_first, panel_second], axis=0)
    height = panels.shape[0]
    order = height * row_devices
    panels_whole = lax.all_gather(panels, "row", axis=0, tiled=True)
    chosen = jnp.concatenate([removed_first, removed_second])[None, :]
    mine = extract(weights, panels, chosen)
    spread = jnp.broadcast_to(mine[None], (col_devices,) + mine.shape)
    received = lax.all_to_all(spread, "col", 0, 0)
    columns, entries = compact(received, rows, height, order)
    entries = jnp.broadcast_to(entries[None], (row_devices,) + entries.shape)
    entries = lax.all_to_all(entries, "row", 0, 0).reshape(order, order)
    high, low = solve(entries, columns)
    return update(weights, panels_whole, high, low)


def solution(mesh):
    return jax.shard_map(
        on_device,
        mesh=mesh,
        in_specs=(P("row", "col"), P("row", "col"), P("row", "col"), P("col"), P("col")),
        out_specs=P("row", "col"),
        check_vma=False,
    )
```

time: 977 us -> 131 us (0.13); the launches traced: 961 us -> 131 us
  waiting for transfers between devices: 657 us -> 3.37 us
  other arithmetic: 111 us -> 1.31 us
  local copies, waits for them, and re-layouts: 47.5 us -> 4.37 us
  matrix products: 35.9 us -> 0 us
  Pallas kernels: 0 us -> 24.4 us
    all_gather x3 -> x1, waiting for transfers between devices: 656 us -> 3.35 us  [on_device(): panels_whole = lax.all_gather(panels, 'row', axis=0, tiled=True)]
    another operation x25 -> x0, other arithmetic: 110 us -> none  [the longest x5 39.6 us: apply_inverse(): return jax.scipy.linalg.cho_solve((factor, True), matrix.T).T]
    all_to_all x0 -> x2, blocking collectives: none -> 84 us  [the longest x1 44.7 us: on_device(): entries = lax.all_to_all(entries, 'row', 0, 0).reshape(order, order)]
    all_gather x2 -> x0, blocking collectives: 76.4 us -> none  [the longest x1 38.7 us: on_device(): second_cols = lax.all_gather(second_local, 'col', axis=1, tiled=True)]
    dot_general x10 -> x0, matrix products: 26.3 us -> none  [the longest x1 8.27 us: on_device(): jnp.dot(coef_first, panel_whole, precision=highest)]
    pallas_call x0 -> x4, Pallas kernels: none -> 24.4 us  [the longest x1 9.72 us: update(): pl.pallas_call(update_kernel, out_shape=jax.ShapeDtypeStruct((rows, width...]
    reshape x3 -> x0, local copies, waits for them, and re-layouts: 16.1 us -> none  [the longest x2 12.2 us: on_device(): everyone.reshape(row_devices, col_devices, 2, panel_rows, 2, slot_count)]
    unnamed x1 -> x0, blocking collectives: 15.6 us -> none
  transfers between devices with their start and end apart: 3 -> 1, of which waited for: 1 -> 1; matrix products, arithmetic and copies ran while one was open for 18% -> 2% of each run, Pallas kernels for 0% -> 11%
where the time goes in v1:
time: 131 us
  blocking collectives  84 us (64%)
  Pallas kernels  24.4 us (19%)
  between operations  13.4 us (10%)
  local copies, waits for them, and re-layouts  4.37 us (3%)
  waiting for transfers between devices  3.37 us (3%)
  other arithmetic  1.31 us (1%)
    all_to_all x1, blocking collectives, on_device(): entries = lax.all_to_all(entries, 'row', 0, 0).reshape(order, order)  44.7 us
    all_to_all x1, blocking collectives, on_device(): received = lax.all_to_all(spread, 'col', 0, 0)  39.3 us
    pallas_call x1, Pallas kernels, update(): pl.pallas_call(update_kernel, out_shape=jax.ShapeDtypeStruct((rows, width...  9.72 us
    pallas_call x1, Pallas kernels, solve(): pl.pallas_call(solve_kernel, out_shape=(jax.ShapeDtypeStruct((rows, order...  8.12 us
    pallas_call x1, Pallas kernels, extract(): pl.pallas_call(extract_kernel, out_shape=jax.ShapeDtypeStruct((total, slo...  3.85 us
    all_gather x1, waiting for transfers between devices, on_device(): panels_whole = lax.all_gather(panels, 'row', axis=0, tiled=True)  3.35 us
    pallas_call x1, Pallas kernels, compact(): pl.pallas_call(compact_kernel, out_shape=(jax.ShapeDtypeStruct((rows, ord...  2.66 us
  transfers between devices with their start and end apart: 1, of which 1 were waited for; matrix products, arithmetic and copies ran while one was open for 2% of the time, Pallas kernels for 11%

profile of v1, /device:TPU:1, one launch (start us, length us, event | category | flops | bytes accessed | tf_op | source)
XLA Modules:
  0.0 130.8 jit_solution(12803657598612870300)
XLA Ops:
  6.5 0.0 all-gather.2.cloned.1.call-start
  6.5 0.9 constant_dynamic-update-slice_fusion.1
  7.5 0.9 constant_dynamic-update-slice_fusion.panels_ref
  8.4 0.0 copy-start
  8.4 0.7 copy-done
  9.1 0.0 all-gather.2.cloned.1.call-update
  9.1 1.3 %add_bitcast_fusion.chosen_ref = s32[1,128]{1,0:T(1,128)} fusion(s32[64]{0:T(128)} %param.9, s32[64]{0:T(128)} %param.8), kind=kLoop, calls=%fused_computation.2 | loop fusion | flops 128 | bytes 1024 | tf_op jit(solution)/shard_map/broadcast_in_dim | solution.py:260
  10.4 3.9 %extract.1 = bf16[320,128]{1,0:T(8,128)(2,1)} custom-call(bf16[256,4096]{1,0:T(8,128)(2,1)} %weights_ref.3, f32[16,4096]{1,0:T(8,128)} %copy-done, s32[1,128]{1,0:T(1,128)} %add_bitcast_fusion.chosen_ref), custom_call_target="tpu_custom_call" | custom-call | tf_op jit(solution)/shard_map/extract/pallas_call | solution.py:70
  14.3 1.0 broadcast_in_dim.7
  15.2 39.3 %all_to_all.10.slots_ref = bf16[8,320,128]{2,1,0:T(8,128)(2,1)} all-to-all(bf16[8,320,128]{2,1,0:T(8,128)(2,1)S(1)} %broadcast_in_dim.7), channel_id=1, replica_groups=mesh['row'=32,'col'=8] {'col'}, dimensions={0} | all-to-all | bytes 1310720 | tf_op jit(solution)/shard_map/all_to_all | solution.py:263
  54.6 2.7 %compact.1 = (bf16[256,512]{1,0:T(8,128)(2,1)}, f32[16,512]{1,0:T(8,128)}) custom-call(bf16[8,320,128]{2,1,0:T(8,128)(2,1)} %all_to_all.10.slots_ref), custom_call_target="tpu_custom_call" | custom-call | tf_op jit(solution)/shard_map/compact/pallas_call | solution.py:130
  57.3 0.9 broadcast_in_dim.8
  58.1 44.7 %all_to_all.11 = f32[32,16,512]{2,1,0:T(8,128)} all-to-all(f32[32,16,512]{2,1,0:T(8,128)S(1)} %broadcast_in_dim.8), channel_id=1, replica_groups=mesh['row'=32,'col'=8] {'row'}, dimensions={0} | all-to-all | bytes 2097152 | tf_op jit(solution)/shard_map/all_to_all | solution.py:266
  102.8 8.1 %solve.1 = (bf16[256,512]{1,0:T(8,128)(2,1)}, bf16[256,512]{1,0:T(8,128)(2,1)}) custom-call(f32[512,512]{1,0:T(8,128)} %bitcast.3, bf16[256,512]{1,0:T(8,128)(2,1)} %get-tuple-element.10.columns_ref), custom_call_target="tpu_custom_call" | custom-call | tf_op jit(solution)/shard_map/solve/pallas_call | solution.py:216
  110.9 3.4 %all-gather.2.cloned.1.call-done.panels_ref = f32[512,4096]{1,0:T(8,128)} async-done(((f32[16,4096]{1,0:T(8,128)}), f32[512,4096]{1,0:T(8,128)}) %all-gather.2.cloned.1.call-update) | async-done | bytes 8388624 | tf_op jit(solution)/shard_map/all_gather | solution.py:259
  114.3 9.7 %update.1 = bf16[256,4096]{1,0:T(8,128)(2,1)} custom-call(bf16[256,4096]{1,0:T(8,128)(2,1)} %weights_ref.3, f32[512,4096]{1,0:T(8,128)} %all-gather.2.cloned.1.call-done.panels_ref, bf16[256,512]{1,0:T(8,128)(2,1)} %get-tuple-element.11.high_ref, bf16[256,512]{1,0:T(8,128)(2,1)} %get-tuple-element.12.low_ref), custom_call_target="tpu_custom_call" | custom-call | tf_op jit(solution)/shard_map/update/pallas_call | solution.py:237
Async XLA Ops:
  6.5 107.7 %all-gather.2.cloned.1.call-start = ((), (), s32[]{:S(2)}) async-start(), calls=%async_computation.2 | async-start | bytes 8650752 | tf_op jit(solution)/shard_map/all_gather | solution.py:259
  8.4 0.7 copy-start
Sparse Core Ops, SparseCore 0:
  9.2 105.0 all-gather.1
